TPU v7x, 512 devices: a whole 4x4x16 slice. The times are simulated.
512 devices in a mesh: wide: 64 (over z, x), narrow: 8 (over y, core).
Axes of the slice: x: 4, y: 4, z: 16, core: 2. Of those that a mesh axis runs over, the one named last changes fastest.
Arguments:
- sublevel_symbol_entries: bfloat16 [1024, 4, 4096], P('wide', None, 'narrow'), may hold values from -160 to 160
- prior_symbol_memory: bfloat16 [1024, 4096], P('wide', 'narrow'), may hold values from -6 to 6
- entry_scaling_multiplier: float32 [4096], P('narrow'), may hold values from 0.25 to 1.75
- entry_scaling_offset: float32 [4096], P('narrow'), may hold values from -4 to 4
- learned_blending: float32 [6, 4096], P(None, 'narrow'), may hold values from 0 to 1
- blending_lowering_coefficients: bfloat16 [4096, 160], P('narrow'), may hold values from -0.09375 to 0.09375
- blending_raising_coefficients: bfloat16 [5, 32, 4096], P(None, None, 'narrow'), may hold values from -1 to 1
- fading_lowering_coefficients: bfloat16 [4096, 64], P('narrow'), may hold values from -0.09375 to 0.09375
- fading_raising_coefficients: bfloat16 [64, 4096], P(None, 'wide'), may hold values from -0.75 to 0.75
- learned_fading: float32 [4096], P('wide'), may hold values from -6 to 1
- immediate_item_premium: float32 [4096], P('wide'), may hold values from -3 to 3
- acceptor_projection: bfloat16 [4096, 4096], P('narrow', 'wide'), may hold values from -0.09375 to 0.09375
- lookup_projection: bfloat16 [4096, 4096], P('narrow', 'wide'), may hold values from -0.09375 to 0.09375
- payload_projection: bfloat16 [4096, 4096], P('narrow', 'wide'), may hold values from -0.09375 to 0.09375
- gating_projection: bfloat16 [4096, 4096], P('narrow', 'wide'), may hold values from -0.09375 to 0.09375
- emission_projection: bfloat16 [4096, 4096], P(None, 'wide'), may hold values from -0.09375 to 0.09375
- group_scaling_multiplier: float32 [4096], P('wide'), may hold values from 0.25 to 1.75
- group_scaling_offset: float32 [4096], P('wide'), may hold values from -4 to 4
- dialogue_group_memory: float32 [262144, 1024], P('wide', 'narrow'), may hold values from -6 to 6
Outputs:
- mixing_output: bfloat16 [1024, 4, 4096], P('narrow', None, 'wide')
- final_state: float32 [262144, 1024], P('wide', 'narrow')
All inputs are finite; a program needn't handle non-finite values.
Results may differ from a plain program's by a relative error of at most 0.034.
Values may be sent and summed in bfloat16 or wider, within the bound.
A program may use at most 64 MiB of HBM per device.

v0:
```python
import jax
import jax.numpy as jnp
from jax import lax
from jax.sharding import PartitionSpec as P

CHANNEL_SPAN = 64
FEATURE_EXTENT = 4096


def per_device(
    sublevel_symbol_entries,
    prior_symbol_memory,
    entry_scaling_multiplier,
    entry_scaling_offset,
    learned_blending,
    blending_lowering_coefficients,
    blending_raising_coefficients,
    fading_lowering_coefficients,
    fading_raising_coefficients,
    learned_fading,
    immediate_item_premium,
    acceptor_projection,
    lookup_projection,
    payload_projection,
    gating_projection,
    emission_projection,
    group_scaling_multiplier,
    group_scaling_offset,
    dialogue_group_memory,
):
    rank = blending_raising_coefficients.shape[1]
    narrow_rows = dialogue_group_memory.shape[1]
    local_width = emission_projection.shape[1]
    group_partition = local_width // CHANNEL_SPAN
    weights = (acceptor_projection, lookup_projection, payload_projection, gating_projection)
    shift_gathered = lax.all_gather(prior_symbol_memory, "wide", axis=0, tiled=True)

    def channel_set_first(block):
        return block.reshape(narrow_rows, group_partition, CHANNEL_SPAN).transpose(1, 2, 0)

    present_symbol = dialogue_group_memory.reshape(
        group_partition, CHANNEL_SPAN, CHANNEL_SPAN, narrow_rows
    )
    previous_rows = prior_symbol_memory
    previous_all = shift_gathered
    results = []
    for index in range(sublevel_symbol_entries.shape[1]):
        floats = sublevel_symbol_entries[:, index : index + 1].astype(jnp.float32)
        totals, squares = lax.psum((jnp.sum(floats, -1), jnp.sum(floats * floats, -1)), "narrow")
        prepare_center = totals[..., None] / FEATURE_EXTENT
        spread = squares[..., None] / FEATURE_EXTENT - prepare_center * prepare_center
        normed = (
            (floats - prepare_center) * lax.rsqrt(spread + 1e-05) * entry_scaling_multiplier
            + entry_scaling_offset
        ).astype(jnp.bfloat16)
        previous = jnp.concatenate([previous_rows[:, None], normed[:, :-1]], 1)
        prepare_normalized_float = normed.astype(jnp.float32)
        prepare_shifted_input = previous.astype(jnp.float32) - prepare_normalized_float
        blended = (prepare_normalized_float + prepare_shifted_input * learned_blending[0]).astype(
            jnp.bfloat16
        )
        partial_mix = jnp.einsum(
            "smd,dr->smr",
            blended,
            blending_lowering_coefficients,
            preferred_element_type=jnp.float32,
        )
        hidden_activation = jnp.tanh(lax.psum(partial_mix, "narrow")).astype(jnp.bfloat16)
        decay_shift = jnp.einsum(
            "smr,rd->smd",
            hidden_activation[..., :rank],
            blending_raising_coefficients[0],
            preferred_element_type=jnp.float32,
        )
        decay_mix = (
            prepare_normalized_float + prepare_shifted_input * (learned_blending[1] + decay_shift)
        ).astype(jnp.bfloat16)
        partial_decay = jnp.einsum(
            "smd,dr->smr",
            decay_mix,
            fading_lowering_coefficients,
            preferred_element_type=jnp.float32,
        )
        decay_hidden = jnp.tanh(lax.psum(partial_decay, "narrow")).astype(jnp.bfloat16)
        small = jnp.concatenate([hidden_activation[..., rank:], decay_hidden], -1)
        prepare_normed_all = lax.all_gather(normed, "wide", axis=0, tiled=True)
        prepare_small_all = lax.all_gather(small, "wide", axis=0, tiled=True)
        normed, normed_all, small_all = (normed, prepare_normed_all, prepare_small_all)
        project_previous_all = previous_all[:, None]
        normalized_float = normed_all.astype(jnp.float32)
        shifted_input = project_previous_all.astype(jnp.float32) - normalized_float
        term_results = []
        for selector_index in range(4):
            low_rank_update = jnp.einsum(
                "smr,rd->smd",
                small_all[..., selector_index * rank : (selector_index + 1) * rank],
                blending_raising_coefficients[selector_index + 1],
                preferred_element_type=jnp.float32,
            )
            mixed_input = (
                normalized_float
                + shifted_input * (learned_blending[selector_index + 2] + low_rank_update)
            ).astype(jnp.bfloat16)
            term_results.append(
                jnp.einsum(
                    "smd,de->sme",
                    mixed_input,
                    weights[selector_index],
                    preferred_element_type=jnp.float32,
                )
            )
        project_transformed_outcome = lax.psum_scatter(
            jnp.concatenate(term_results, -1).astype(jnp.bfloat16),
            "narrow",
            scatter_dimension=0,
            tiled=True,
        ).astype(jnp.float32)
        rows_start = lax.axis_index("narrow") * narrow_rows
        decay_rows = lax.dynamic_slice_in_dim(
            small_all[..., 4 * rank :], rows_start, narrow_rows, 0
        )
        decay_log = learned_fading + jnp.einsum(
            "smr,rd->smd",
            decay_rows,
            fading_raising_coefficients,
            preferred_element_type=jnp.float32,
        )
        shrink_coefficient = jnp.exp(-jnp.exp(decay_log))
        recurrence_present_symbol = present_symbol
        each_group_reward = immediate_item_premium.reshape(group_partition, CHANNEL_SPAN)
        present_acceptor = channel_set_first(project_transformed_outcome[:, 0, :local_width])
        key_now = channel_set_first(
            project_transformed_outcome[:, 0, local_width : 2 * local_width]
        )
        value_now = channel_set_first(
            project_transformed_outcome[:, 0, 2 * local_width : 3 * local_width]
        )
        gate_now = project_transformed_outcome[:, 0, 3 * local_width :]
        forget_now = channel_set_first(shrink_coefficient[:, 0])
        dyadic_tensor = key_now[:, :, None, :] * value_now[:, None, :, :]
        memory_retrieval = jnp.sum(
            present_acceptor[:, :, None, :]
            * (recurrence_present_symbol + each_group_reward[:, :, None, None] * dyadic_tensor),
            1,
        )
        recurrence_present_symbol = (
            forget_now[:, :, None, :] * recurrence_present_symbol + dyadic_tensor
        )
        center = jnp.mean(memory_retrieval, 1, keepdims=True)
        offset = memory_retrieval - center
        scaled = offset * lax.rsqrt(jnp.mean(offset * offset, 1, keepdims=True) + 0.00064)
        squashed_vector = scaled.transpose(2, 0, 1).reshape(narrow_rows, local_width)
        pieces = [
            (
                (squashed_vector * group_scaling_multiplier + group_scaling_offset)
                * jax.nn.silu(gate_now)
            ).astype(jnp.bfloat16)
        ]
        present_symbol = recurrence_present_symbol
        gated = jnp.stack(pieces, 1)
        results.append(
            jnp.einsum(
                "smc,ce->sme",
                lax.all_gather(gated, "wide", axis=2, tiled=True),
                emission_projection,
                preferred_element_type=jnp.float32,
            ).astype(jnp.bfloat16)
        )
        previous_rows = normed[:, 0]
        previous_all = normed_all[:, 0]
    mixing_output = jnp.concatenate(results, 1)
    return (
        mixing_output,
        present_symbol.reshape(group_partition * CHANNEL_SPAN * CHANNEL_SPAN, narrow_rows),
    )


def solution(mesh):
    placed = (
        P("wide", None, "narrow"),
        P("wide", "narrow"),
        P("narrow"),
        P("narrow"),
        P(None, "narrow"),
        P("narrow", None),
        P(None, None, "narrow"),
        P("narrow", None),
        P(None, "wide"),
        P("wide"),
        P("wide"),
        P("narrow", "wide"),
        P("narrow", "wide"),
        P("narrow", "wide"),
        P("narrow", "wide"),
        P(None, "wide"),
        P("wide"),
        P("wide"),
        P("wide", "narrow"),
    )
    return jax.shard_map(
        per_device,
        mesh=mesh,
        in_specs=placed,
        out_specs=(P("narrow", None, "wide"), P("wide", "narrow")),
        check_vma=False,
    )
```

profile of v0, /device:TPU:8, one launch (start us, length us, event | category | flops | bytes accessed | tf_op | source)
XLA Modules:
  0.0 1447.9 jit_solution(15403730953367358589)
XLA Ops:
  7.3 1.1 fusion.287
  8.7 14.8 %all-reduce.2 = (f32[16,1]{0,1:T(1,128)S(1)}, f32[16,1]{0,1:T(1,128)S(1)}, f32[16,1]{0,1:T(1,128)S(1)}, f32[16,1]{0,1:T(1,128)S(1)}, f32[16,1]{0,1:T(1,128)S(1)}...) all-reduce(f32[16,1]{0,1:T(1,128)S(1)} %bitcast.846, ...), channel_id=1, replica_groups=mesh['wide'=64,'narrow'=8] {'narrow'}, use_global_device_ids=true, to_apply=%region_13.14 | all-reduce | flops 128 | bytes 1024 | tf_op jit(solution)/shard_map/psum | solution.py:49
  23.6 1.4 fusion.145
  25.0 0.7 all-gather.20.cloned.1.call-update
  27.7 1.0 fusion.288
  28.6 1.1 convolution_bitcast_fusion
  29.7 1.1 convolution_bitcast_fusion.1
  30.9 1.1 convolution_bitcast_fusion.2
  32.0 1.1 convolution_bitcast_fusion.3
  33.1 24.0 %all-reduce.1 = (f32[16,1,160]{2,0,1:T(8,128)S(1)}, f32[16,1,160]{2,0,1:T(8,128)S(1)}, f32[16,1,160]{2,0,1:T(8,128)S(1)}, f32[16,1,160]{2,0,1:T(8,128)S(1)}) all-reduce(f32[16,1,160]{2,0,1:T(8,128)S(1)} %convolution_bitcast_fusion.1, ...), channel_id=1, replica_groups=mesh['wide'=64,'narrow'=8] {'narrow'}, use_global_device_ids=true, to_apply=%region_24.25 | all-reduce | flops 10240 | bytes 81920 | tf_op jit(solution)/shard_map/psum | solution.py:68
  57.2 1.1 convolution_bitcast_fusion.5
  58.3 1.1 convolution_bitcast_fusion.6
  59.5 1.0 convolution_bitcast_fusion.7
  60.6 1.0 convolution_bitcast_fusion.4
  61.9 24.4 %all-reduce = (f32[16,1,64]{2,0,1:T(8,128)S(1)}, f32[16,1,64]{2,0,1:T(8,128)S(1)}, f32[16,1,64]{2,0,1:T(8,128)S(1)}, f32[16,1,64]{2,0,1:T(8,128)S(1)}) all-reduce(f32[16,1,64]{2,0,1:T(8,128)S(1)} %convolution_bitcast_fusion.5, f32[16,1,64]{2,0,1:T(8,128)S(1)} %convolution_bitcast_fusion.6, ...), channel_id=1, replica_groups=mesh['wide'=64,'narrow'=8] {'narrow'}, use_global_device_ids=true, to_apply=%region_25.26 | all-reduce | flops 4096 | bytes 32768 | tf_op jit(solution)/shard_map/psum | solution.py:84
  86.4 103.3 %all_gather.50 = bf16[1024,1,192]{2,0,1:T(8,128)(2,1)S(1)} all-gather(bf16[16,1,192]{2,0,1:T(8,128)(2,1)S(1)} %pad_maximum_fusion.4), channel_id=1, replica_groups=mesh['wide'=64,'narrow'=8] {'wide'}, dimensions={0}, use_global_device_ids=true | all-gather | bytes 399360 | tf_op jit(solution)/shard_map/all_gather | solution.py:87
  189.7 99.2 %all_gather.41 = bf16[1024,1,192]{2,0,1:T(8,128)(2,1)S(1)} all-gather(bf16[16,1,192]{2,0,1:T(8,128)(2,1)S(1)} %pad_maximum_fusion.1), channel_id=1, replica_groups=mesh['wide'=64,'narrow'=8] {'wide'}, dimensions={0}, use_global_device_ids=true | all-gather | bytes 399360 | tf_op jit(solution)/shard_map/all_gather | solution.py:87
  288.9 97.0 %all_gather.44 = bf16[1024,1,192]{2,0,1:T(8,128)(2,1)S(1)} all-gather(bf16[16,1,192]{2,0,1:T(8,128)(2,1)S(1)} %pad_maximum_fusion.2), channel_id=1, replica_groups=mesh['wide'=64,'narrow'=8] {'wide'}, dimensions={0}, use_global_device_ids=true | all-gather | bytes 399360 | tf_op jit(solution)/shard_map/all_gather | solution.py:87
  385.9 99.0 %all_gather.47 = bf16[1024,1,192]{2,0,1:T(8,128)(2,1)S(1)} all-gather(bf16[16,1,192]{2,0,1:T(8,128)(2,1)S(1)} %pad_maximum_fusion.3), channel_id=1, replica_groups=mesh['wide'=64,'narrow'=8] {'wide'}, dimensions={0}, use_global_device_ids=true | all-gather | bytes 399360 | tf_op jit(solution)/shard_map/all_gather | solution.py:87
  484.9 0.7 slice.308
  486.3 1.0 fusion.83
  487.3 2.4 fusion.75
  489.7 2.4 fusion.74
  492.2 2.3 fusion.73
  494.5 2.3 fusion.72
  496.8 1.0 copy.43
  498.1 81.7 %all-gather.10.cloned.1.call-done = bf16[1024,1,512]{2,0,1:T(8,128)(2,1)} async-done(((bf16[16,1,512]{2,0,1:T(8,128)(2,1)}), bf16[1024,1,512]{2,0,1:T(8,128)(2,1)}) %all-gather.10.cloned.1.call-update) | async-done | bytes 1048592 | tf_op jit(solution)/shard_map/all_gather | solution.py:86
  579.9 2.4 fusion.63
  582.3 2.4 fusion.62
  584.7 2.4 fusion.61
  587.1 2.3 fusion.60
  589.4 1.0 copy.37
  590.5 127.2 %all-gather.16.cloned.1.call-done = bf16[1024,1,512]{2,0,1:T(8,128)(2,1)} async-done(((bf16[16,1,512]{2,0,1:T(8,128)(2,1)}), bf16[1024,1,512]{2,0,1:T(8,128)(2,1)}) %all-gather.16.cloned.1.call-update) | async-done | bytes 1048592 | tf_op jit(solution)/shard_map/all_gather | solution.py:86
  717.7 2.4 fusion.67
  720.2 2.1 fusion.66
  722.2 2.0 fusion.65
  724.3 2.0 fusion.64
  726.3 1.0 copy.39
  727.6 2.1 fusion.71
  729.7 2.1 fusion.70
  731.8 2.1 fusion.69
  733.9 2.0 fusion.68
  735.9 1.0 copy.41
  737.2 14.9 %reduce-scatter.19.cloned.1.call-done = bf16[128,256]{1,0:T(8,128)(2,1)} async-done(((bf16[1024,256]{1,0:T(8,128)(2,1)}), bf16[128,256]{1,0:T(8,128)(2,1)}) %reduce-scatter.19.cloned.1.call-update) | async-done | bytes 65552
  752.0 0.9 copy.44
  753.0 39.6 %reduce-scatter.13.cloned.1.call-done = bf16[128,256]{1,0:T(8,128)(2,1)} async-done(((bf16[1024,256]{1,0:T(8,128)(2,1)}), bf16[128,256]{1,0:T(8,128)(2,1)}) %reduce-scatter.13.cloned.1.call-update) | async-done | bytes 65552
  792.7 0.9 copy.38
  793.6 39.4 %reduce-scatter.15.cloned.1.call-done = bf16[128,256]{1,0:T(8,128)(2,1)} async-done(((bf16[1024,256]{1,0:T(8,128)(2,1)}), bf16[128,256]{1,0:T(8,128)(2,1)}) %reduce-scatter.15.cloned.1.call-update) | async-done | bytes 65552
  833.0 0.9 copy.40
  834.0 40.1 %reduce-scatter.17.cloned.1.call-done = bf16[128,256]{1,0:T(8,128)(2,1)} async-done(((bf16[1024,256]{1,0:T(8,128)(2,1)}), bf16[128,256]{1,0:T(8,128)(2,1)}) %reduce-scatter.17.cloned.1.call-update) | async-done | bytes 65552
  874.2 0.9 copy.42
  876.2 1.1 copy-done.1
  877.3 2.1 fusion.8
  879.4 1.9 fusion.28
  881.3 2.1 fusion.43
  883.6 0.7 fusion.168
  886.4 138.9 %all-gather.14.cloned.1.call-done = bf16[128,1,4096]{0,2,1:T(8,128)(2,1)} async-done(((bf16[128,1,64]{0,2,1:T(8,128)(2,1)}), bf16[128,1,4096]{0,2,1:T(8,128)(2,1)}) %all-gather.14.cloned.1.call-update) | async-done | bytes 1048592 | tf_op jit(solution)/shard_map/all_gather | solution.py:164
  1025.4 1.5 fusion.108
  1026.9 136.4 %all-gather.18.cloned.1.call-done = bf16[128,1,4096]{0,2,1:T(8,128)(2,1)} async-done(((bf16[128,1,64]{0,2,1:T(8,128)(2,1)}), bf16[128,1,4096]{0,2,1:T(8,128)(2,1)}) %all-gather.18.cloned.1.call-update) | async-done | bytes 1048592 | tf_op jit(solution)/shard_map/all_gather | solution.py:164
  1163.4 1.5 fusion.109
  1164.9 136.3 %all-gather.22.cloned.1.call-done = bf16[128,1,4096]{0,2,1:T(8,128)(2,1)} async-done(((bf16[128,1,64]{0,2,1:T(8,128)(2,1)}), bf16[128,1,4096]{0,2,1:T(8,128)(2,1)}) %all-gather.22.cloned.1.call-update) | async-done | bytes 1048592 | tf_op jit(solution)/shard_map/all_gather | solution.py:164
  1301.2 1.5 fusion.110
  1302.7 136.4 %all-gather.26.cloned.1.call-done = bf16[128,1,4096]{0,2,1:T(8,128)(2,1)} async-done(((bf16[128,1,64]{0,2,1:T(8,128)(2,1)}), bf16[128,1,4096]{0,2,1:T(8,128)(2,1)}) %all-gather.26.cloned.1.call-update) | async-done | bytes 1048592 | tf_op jit(solution)/shard_map/all_gather | solution.py:164
  1439.2 1.5 fusion.111
  (130 shorter events, 8.6 us)
Async XLA Ops:
  7.2 1018.2 %copy-start = (bf16[4096,64]{0,1:T(8,128)(2,1)S(1)}, bf16[4096,64]{0,1:T(8,128)(2,1)}, u32[]{:S(2)}) copy-start(bf16[4096,64]{0,1:T(8,128)(2,1)} %param.34) | copy-start | bytes 1572868
  7.2 52.3 %copy-start.4 = (bf16[16,512]{1,0:T(8,128)(2,1)S(1)}, bf16[16,512]{1,0:T(8,128)(2,1)}, u32[]{:S(2)}) copy-start(bf16[16,512]{1,0:T(8,128)(2,1)} %param.20) | copy-start | bytes 49156
  7.2 52.3 %copy-start.2 = (bf16[512,64]{0,1:T(8,128)(2,1)S(1)}, bf16[512,64]{0,1:T(8,128)(2,1)}, u32[]{:S(2)}) copy-start(bf16[512,64]{0,1:T(8,128)(2,1)} %param.26) | copy-start | bytes 196612
  7.2 54.5 %copy-start.7 = (f32[64]{0:T(128)S(1)}, f32[64]{0:T(128)}, u32[]{:S(2)}) copy-start(f32[64]{0:T(128)} %param.29) | copy-start | bytes 772
  7.2 480.1 %all-gather.24.cloned.1.call-start = ((), (), s32[]{:S(2)}) async-start(), calls=%async_computation.11 | async-start | bytes 1064960 | tf_op jit(solution)/shard_map/all_gather | solution.py:86
  25.0 462.3 %all-gather.20.cloned.1.call-start = ((), (), s32[]{:S(2)}) async-start(), calls=%async_computation.9 | async-start | bytes 1064960 | tf_op jit(solution)/shard_map/all_gather | solution.py:86
  25.7 472.4 %all-gather.12.cloned.1.call-start = ((), (), s32[]{:S(2)}) async-start(), calls=%async_computation.5 | async-start | bytes 1064960 | tf_op jit(solution)/shard_map/all_gather | solution.py:36
  26.5 553.4 %all-gather.10.cloned.1.call-start = ((), (), s32[]{:S(2)}) async-start(), calls=%async_computation.4 | async-start | bytes 1064960 | tf_op jit(solution)/shard_map/all_gather | solution.py:86
  27.1 690.7 %all-gather.16.cloned.1.call-start = ((), (), s32[]{:S(2)}) async-start(), calls=%async_computation.7 | async-start | bytes 1064960 | tf_op jit(solution)/shard_map/all_gather | solution.py:86
  27.6 724.4 %reduce-scatter.19.cloned.1.call-start = ((), (), s32[]{:S(2)}) async-start(), calls=%async_computation.16 | async-start | bytes 589824
  86.3 399.3 %copy-start.3 = (bf16[64,64]{1,0:T(8,128)(2,1)S(1)}, bf16[64,64]{1,0:T(8,128)(2,1)}, u32[]{:S(2)}) copy-start(bf16[64,64]{1,0:T(8,128)(2,1)} %param.27) | copy-start | bytes 24580
  86.4 399.3 %copy-start.6 = (f32[64]{0:T(128)S(1)}, f32[64]{0:T(128)}, u32[]{:S(2)}) copy-start(f32[64]{0:T(128)} %param.28) | copy-start | bytes 772
  489.7 2.5 copy-start.5
  489.7 2.5 copy-start.15
  497.8 84.4 %copy-start.13 = (bf16[512,64]{0,1:T(8,128)(2,1)S(1)}, bf16[512,64]{0,1:T(8,128)(2,1)}, u32[]{:S(2)}) copy-start(bf16[512,64]{0,1:T(8,128)(2,1)} %param.32) | copy-start | bytes 196612
  497.9 294.8 %reduce-scatter.13.cloned.1.call-start = ((), (), s32[]{:S(2)}) async-start(), calls=%async_computation.13 | async-start | bytes 589824
  582.2 2.4 copy-start.16
  584.7 2.4 copy-start.18
  589.4 128.4 %copy-start.12 = (bf16[512,64]{0,1:T(8,128)(2,1)S(1)}, bf16[512,64]{0,1:T(8,128)(2,1)}, u32[]{:S(2)}) copy-start(bf16[512,64]{0,1:T(8,128)(2,1)} %param.33) | copy-start | bytes 196612
  590.4 242.6 %reduce-scatter.15.cloned.1.call-start = ((), (), s32[]{:S(2)}) async-start(), calls=%async_computation.14 | async-start | bytes 589824
  717.7 2.5 copy-start.11
  726.2 1.3 copy-start.10
  727.3 2.3 copy-start.14
  727.3 146.8 %reduce-scatter.17.cloned.1.call-start = ((), (), s32[]{:S(2)}) async-start(), calls=%async_computation.15 | async-start | bytes 589824
  729.6 2.1 copy-start.17
  731.7 2.1 copy-start.19
  736.9 288.5 %all-gather.14.cloned.1.call-start = ((), (), s32[]{:S(2)}) async-start(), calls=%async_computation.6 | async-start | bytes 1064960 | tf_op jit(solution)/shard_map/all_gather | solution.py:164
  875.7 1.6 copy-start.1
  881.3 2.3 copy-start.8
  881.3 2.3 copy-start.9
  884.4 279.0 %all-gather.18.cloned.1.call-start = ((), (), s32[]{:S(2)}) async-start(), calls=%async_computation.8 | async-start | bytes 1064960 | tf_op jit(solution)/shard_map/all_gather | solution.py:164
  885.1 416.1 %all-gather.22.cloned.1.call-start = ((), (), s32[]{:S(2)}) async-start(), calls=%async_computation.10 | async-start | bytes 1064960 | tf_op jit(solution)/shard_map/all_gather | solution.py:164
  885.7 553.5 %all-gather.26.cloned.1.call-start = ((), (), s32[]{:S(2)}) async-start(), calls=%async_computation.12 | async-start | bytes 1064960 | tf_op jit(solution)/shard_map/all_gather | solution.py:164
Sparse Core Ops, SparseCore 0:
  25.1 140.8 all-gather.23
  168.9 134.9 all-gather.19
  306.8 135.0 all-gather.11
  444.7 135.1 all-gather.9
  582.7 134.9 all-gather.15
  720.4 31.6 reduce-scatter.18
  755.1 37.5 reduce-scatter.12
  795.5 37.4 reduce-scatter.14
  836.6 37.5 reduce-scatter.16
  884.5 140.8 all-gather.13
  1028.3 134.9 all-gather.17
  1166.2 134.9 all-gather.21
  1304.1 134.9 all-gather.25
where the time goes:
time: 1450 us
  waiting for transfers between devices  896 us (62%)
  blocking collectives  462 us (32%)
  matrix products  51.9 us (4%)
  between operations  14.7 us (1%)
    all_gather x4, waiting for transfers between devices, per_device(): lax.all_gather(gated, 'wide', axis=2, tiled=True)  548 us
    all_gather x4, blocking collectives, per_device(): prepare_small_all = lax.all_gather(small, 'wide', axis=0, tiled=True)  398 us
    all_gather x4, waiting for transfers between devices, per_device(): prepare_normed_all = lax.all_gather(normed, 'wide', axis=0, tiled=True)  209 us
    unnamed x17, waiting for transfers between devices  138 us
    dot_general x16, matrix products, per_device(): jnp.einsum('smd,de->sme', mixed_input, weights[selector_index], preferred...  35.5 us
  transfers between devices with their start and end apart: 13, of which 10 were waited for; matrix products, arithmetic and copies ran while one was open for 4% of the time, Pallas kernels for 0%

commit v1 on v0

--- a/solution.py
+++ b/solution.py
@@ -2,9 +2,22 @@
 import jax.numpy as jnp
 from jax import lax
 from jax.sharding import PartitionSpec as P
+from jax.lax import all_to_all, axis_size
 
 CHANNEL_SPAN = 64
 FEATURE_EXTENT = 4096
+
+
+def _prepare_stocks(state, comm_axis, join_dim=2):
+    return jnp.concatenate(
+        all_to_all(
+            jnp.stack(axis_size(comm_axis) * [state], axis=0),
+            axis_name=comm_axis,
+            split_axis=0,
+            concat_axis=0,
+        ),
+        axis=join_dim,
+    )
 
 
 def per_device(
@@ -161,7 +174,7 @@
         results.append(
             jnp.einsum(
                 "smc,ce->sme",
-                lax.all_gather(gated, "wide", axis=2, tiled=True),
+                _prepare_stocks(gated, "wide"),
                 emission_projection,
                 preferred_element_type=jnp.float32,
             ).astype(jnp.bfloat16)

time: 1450 us -> 1140 us (0.79)
  the two profiles are of different devices: /device:TPU:8 before, /device:TPU:24 now
where the time goes in v1:
time: 1140 us
  blocking collectives  653 us (57%)
  waiting for transfers between devices  386 us (34%)
  matrix products  49.4 us (4%)
  local copies, waits for them, and re-layouts  16.1 us (1%)
  between operations  14.7 us (1%)
    all_gather x4, blocking collectives, per_device(): prepare_small_all = lax.all_gather(small, 'wide', axis=0, tiled=True)  398 us
    all_to_all x3, blocking collectives, _prepare_stocks(): all_to_all(jnp.stack(axis_size(comm_axis) * [state], axis=0), axis_name=c...  193 us
    all_gather x4, waiting for transfers between devices, per_device(): prepare_normed_all = lax.all_gather(normed, 'wide', axis=0, tiled=True)  187 us
    unnamed x13, waiting for transfers between devices  146 us
    all_to_all x1, waiting for transfers between devices, _prepare_stocks(): all_to_all(jnp.stack(axis_size(comm_axis) * [state], axis=0), axis_name=c...  52 us
    dot_general x16, matrix products, per_device(): jnp.einsum('smd,de->sme', mixed_input, weights[selector_index], preferred...  36.6 us
    psum x1, blocking collectives, per_device(): lax.psum(partial_mix, 'narrow')  24.5 us
    psum x1, blocking collectives, per_device(): lax.psum(partial_decay, 'narrow')  23.3 us
  transfers between devices with their start and end apart: 10, of which 7 were waited for; matrix products, arithmetic and copies ran while one was open for 5% of the time, Pallas kernels for 0%

profile of v1, /device:TPU:24, one launch (start us, length us, event | category | flops | bytes accessed | tf_op | source)
XLA Modules:
  0.0 1135.9 jit_solution(3230499768780510935)
XLA Ops:
  7.3 0.7 all-gather.8.cloned.1.call-update
  8.0 1.1 fusion.287
  9.4 14.1 %all-reduce.2 = (f32[16,1]{0,1:T(1,128)S(1)}, f32[16,1]{0,1:T(1,128)S(1)}, f32[16,1]{0,1:T(1,128)S(1)}, f32[16,1]{0,1:T(1,128)S(1)}, f32[16,1]{0,1:T(1,128)S(1)}...) all-reduce(f32[16,1]{0,1:T(1,128)S(1)} %bitcast.886, ...), channel_id=1, replica_groups=mesh['wide'=64,'narrow'=8] {'narrow'}, use_global_device_ids=true, to_apply=%region_23.24 | all-reduce | flops 128 | bytes 1024 | tf_op jit(solution)/shard_map/psum | solution.py:62
  23.6 1.4 fusion.126
  25.1 0.7 all-gather.10.cloned.1.call-update
  27.0 1.5 fusion.288
  28.5 1.1 convolution_bitcast_fusion
  29.6 1.1 convolution_bitcast_fusion.3
  30.7 1.1 convolution_bitcast_fusion.2
  31.8 1.1 convolution_bitcast_fusion.1
  32.9 24.5 %all-reduce.1 = (f32[16,1,160]{2,0,1:T(8,128)S(1)}, f32[16,1,160]{2,0,1:T(8,128)S(1)}, f32[16,1,160]{2,0,1:T(8,128)S(1)}, f32[16,1,160]{2,0,1:T(8,128)S(1)}) all-reduce(f32[16,1,160]{2,0,1:T(8,128)S(1)} %convolution_bitcast_fusion, ...), channel_id=1, replica_groups=mesh['wide'=64,'narrow'=8] {'narrow'}, use_global_device_ids=true, to_apply=%region_34.35 | all-reduce | flops 10240 | bytes 81920 | tf_op jit(solution)/shard_map/psum | solution.py:81
  57.6 1.1 convolution_bitcast_fusion.4
  58.7 1.1 convolution_bitcast_fusion.5
  59.9 1.0 convolution_bitcast_fusion.6
  61.0 1.0 convolution_bitcast_fusion.7
  62.2 0.7 mul.863
  62.9 23.3 %all-reduce = (f32[16,1,64]{2,0,1:T(8,128)S(1)}, f32[16,1,64]{2,0,1:T(8,128)S(1)}, f32[16,1,64]{2,0,1:T(8,128)S(1)}, f32[16,1,64]{2,0,1:T(8,128)S(1)}) all-reduce(f32[16,1,64]{2,0,1:T(8,128)S(1)} %convolution_bitcast_fusion.4, f32[16,1,64]{2,0,1:T(8,128)S(1)} %convolution_bitcast_fusion.5, ...), channel_id=1, replica_groups=mesh['wide'=64,'narrow'=8] {'narrow'}, use_global_device_ids=true, to_apply=%region_35.36 | all-reduce | flops 4096 | bytes 32768 | tf_op jit(solution)/shard_map/psum | solution.py:97
  86.2 103.5 %all_gather.29 = bf16[1024,1,192]{2,0,1:T(8,128)(2,1)S(1)} all-gather(bf16[16,1,192]{2,0,1:T(8,128)(2,1)S(1)} %pad_maximum_fusion.1), channel_id=1, replica_groups=mesh['wide'=64,'narrow'=8] {'wide'}, dimensions={0}, use_global_device_ids=true | all-gather | bytes 399360 | tf_op jit(solution)/shard_map/all_gather | solution.py:100
  189.8 98.7 %all_gather.31 = bf16[1024,1,192]{2,0,1:T(8,128)(2,1)S(1)} all-gather(bf16[16,1,192]{2,0,1:T(8,128)(2,1)S(1)} %pad_maximum_fusion.2), channel_id=1, replica_groups=mesh['wide'=64,'narrow'=8] {'wide'}, dimensions={0}, use_global_device_ids=true | all-gather | bytes 399360 | tf_op jit(solution)/shard_map/all_gather | solution.py:100
  288.5 97.4 %all_gather.33 = bf16[1024,1,192]{2,0,1:T(8,128)(2,1)S(1)} all-gather(bf16[16,1,192]{2,0,1:T(8,128)(2,1)S(1)} %pad_maximum_fusion.3), channel_id=1, replica_groups=mesh['wide'=64,'narrow'=8] {'wide'}, dimensions={0}, use_global_device_ids=true | all-gather | bytes 399360 | tf_op jit(solution)/shard_map/all_gather | solution.py:100
  385.9 98.7 %all_gather.35 = bf16[1024,1,192]{2,0,1:T(8,128)(2,1)S(1)} all-gather(bf16[16,1,192]{2,0,1:T(8,128)(2,1)S(1)} %pad_maximum_fusion.4), channel_id=1, replica_groups=mesh['wide'=64,'narrow'=8] {'wide'}, dimensions={0}, use_global_device_ids=true | all-gather | bytes 399360 | tf_op jit(solution)/shard_map/all_gather | solution.py:100
  484.6 0.7 slice.312
  486.0 1.0 fusion.79
  487.0 2.4 fusion.63
  489.5 2.4 fusion.62
  492.0 2.4 fusion.61
  494.3 2.3 fusion.60
  496.7 1.0 copy.49
  498.0 2.3 fusion.67
  500.4 2.4 fusion.66
  502.8 2.4 fusion.65
  505.2 2.3 fusion.64
  507.5 1.0 copy.51
  508.6 60.1 %all-gather.12.cloned.1.call-done = bf16[1024,1,512]{2,0,1:T(8,128)(2,1)} async-done(((bf16[16,1,512]{2,0,1:T(8,128)(2,1)}), bf16[1024,1,512]{2,0,1:T(8,128)(2,1)}) %all-gather.12.cloned.1.call-update) | async-done | bytes 1048592 | tf_op jit(solution)/shard_map/all_gather | solution.py:99
  568.7 2.4 fusion.71
  571.0 2.4 fusion.70
  573.4 2.4 fusion.69
  575.8 2.3 fusion.68
  578.1 1.0 copy.53
  579.2 127.3 %all-gather.14.cloned.1.call-done = bf16[1024,1,512]{2,0,1:T(8,128)(2,1)} async-done(((bf16[16,1,512]{2,0,1:T(8,128)(2,1)}), bf16[1024,1,512]{2,0,1:T(8,128)(2,1)}) %all-gather.14.cloned.1.call-update) | async-done | bytes 1048592 | tf_op jit(solution)/shard_map/all_gather | solution.py:99
  706.5 2.4 fusion.75
  708.9 2.1 fusion.74
  710.9 2.0 fusion.73
  713.0 2.0 fusion.72
  715.0 1.0 copy.55
  716.0 25.4 %reduce-scatter.13.cloned.1.call-done = bf16[128,256]{1,0:T(8,128)(2,1)} async-done(((bf16[1024,256]{1,0:T(8,128)(2,1)}), bf16[128,256]{1,0:T(8,128)(2,1)}) %reduce-scatter.13.cloned.1.call-update) | async-done | bytes 65552
  741.4 0.9 copy.50
  742.4 39.6 %reduce-scatter.15.cloned.1.call-done = bf16[128,256]{1,0:T(8,128)(2,1)} async-done(((bf16[1024,256]{1,0:T(8,128)(2,1)}), bf16[128,256]{1,0:T(8,128)(2,1)}) %reduce-scatter.15.cloned.1.call-update) | async-done | bytes 65552
  782.0 0.9 copy.52
  783.0 39.4 %reduce-scatter.17.cloned.1.call-done = bf16[128,256]{1,0:T(8,128)(2,1)} async-done(((bf16[1024,256]{1,0:T(8,128)(2,1)}), bf16[128,256]{1,0:T(8,128)(2,1)}) %reduce-scatter.17.cloned.1.call-update) | async-done | bytes 65552
  822.4 0.9 copy.54
  823.4 39.6 %reduce-scatter.19.cloned.1.call-done = bf16[128,256]{1,0:T(8,128)(2,1)} async-done(((bf16[1024,256]{1,0:T(8,128)(2,1)}), bf16[128,256]{1,0:T(8,128)(2,1)}) %reduce-scatter.19.cloned.1.call-update) | async-done | bytes 65552
  863.0 0.9 copy.56
  865.0 1.0 copy-done.1
  866.1 2.1 fusion.8
  868.2 1.9 fusion.28
  870.1 2.1 fusion.43
  872.8 72.0 %all_to_all.20 = bf16[64,128,1,64]{1,3,2,0:T(8,128)(2,1)S(1)} all-to-all(bf16[64,128,1,64]{1,3,2,0:T(8,128)(2,1)S(1)} %stack.12), channel_id=1, replica_groups=mesh['wide'=64,'narrow'=8] {'wide'}, dimensions={0} | all-to-all | bytes 2097152 | tf_op jit(solution)/shard_map/all_to_all | solution.py:13
  945.0 60.6 %all_to_all.21 = bf16[64,128,1,64]{1,3,2,0:T(8,128)(2,1)S(1)} all-to-all(bf16[64,128,1,64]{1,3,2,0:T(8,128)(2,1)S(1)} %stack.13), channel_id=1, replica_groups=mesh['wide'=64,'narrow'=8] {'wide'}, dimensions={0} | all-to-all | bytes 2097152 | tf_op jit(solution)/shard_map/all_to_all | solution.py:13
  1005.9 60.4 %all_to_all.22 = bf16[64,128,1,64]{1,3,2,0:T(8,128)(2,1)} all-to-all(bf16[64,128,1,64]{1,3,2,0:T(8,128)(2,1)S(1)} %stack.14), channel_id=1, replica_groups=mesh['wide'=64,'narrow'=8] {'wide'}, dimensions={0} | all-to-all | bytes 2097152 | tf_op jit(solution)/shard_map/all_to_all | solution.py:13
  1066.2 1.3 stack.15
  1067.5 6.1 all-to-all-start.3
  1075.2 52.0 %all-to-all-done.3 = bf16[64,128,1,64]{1,3,2,0:T(8,128)(2,1)} async-done(((bf16[64,128,1,64]{1,3,2,0:T(8,128)(2,1)}), bf16[64,128,1,64]{1,3,2,0:T(8,128)(2,1)}, u32[]{:S(2)}, u32[]{:S(2)}) %all-to-all-start.3) | async-done | bytes 1048608 | tf_op jit(solution)/shard_map/all_to_all | solution.py:13
  1127.2 1.5 fusion.111
  (135 shorter events, 7.8 us)
Async XLA Ops:
  7.2 1066.5 %copy-start = (bf16[4096,64]{0,1:T(8,128)(2,1)S(1)}, bf16[4096,64]{0,1:T(8,128)(2,1)}, u32[]{:S(2)}) copy-start(bf16[4096,64]{0,1:T(8,128)(2,1)} %param.34) | copy-start | bytes 1572868
  7.2 53.8 %copy-start.5 = (bf16[16,512]{1,0:T(8,128)(2,1)S(1)}, bf16[16,512]{1,0:T(8,128)(2,1)}, u32[]{:S(2)}) copy-start(bf16[16,512]{1,0:T(8,128)(2,1)} %param.20) | copy-start | bytes 49156
  7.2 52.7 %copy-start.3 = (bf16[512,64]{0,1:T(8,128)(2,1)S(1)}, bf16[512,64]{0,1:T(8,128)(2,1)}, u32[]{:S(2)}) copy-start(bf16[512,64]{0,1:T(8,128)(2,1)} %param.26) | copy-start | bytes 196612
  7.2 54.9 %copy-start.9 = (f32[64]{0:T(128)S(1)}, f32[64]{0:T(128)}, u32[]{:S(2)}) copy-start(f32[64]{0:T(128)} %param.29) | copy-start | bytes 772
  7.2 479.8 %all-gather.8.cloned.1.call-start = ((), (), s32[]{:S(2)}) async-start(), calls=%async_computation.9 | async-start | bytes 1064960 | tf_op jit(solution)/shard_map/all_gather | solution.py:49
  7.9 479.1 %all-gather.6.cloned.1.call-start = ((), (), s32[]{:S(2)}) async-start(), calls=%async_computation.8 | async-start | bytes 1064960 | tf_op jit(solution)/shard_map/all_gather | solution.py:99
  25.0 472.9 %all-gather.10.cloned.1.call-start = ((), (), s32[]{:S(2)}) async-start(), calls=%async_computation.10 | async-start | bytes 1064960 | tf_op jit(solution)/shard_map/all_gather | solution.py:99
  25.8 542.9 %all-gather.12.cloned.1.call-start = ((), (), s32[]{:S(2)}) async-start(), calls=%async_computation.11 | async-start | bytes 1064960 | tf_op jit(solution)/shard_map/all_gather | solution.py:99
  26.3 680.2 %all-gather.14.cloned.1.call-start = ((), (), s32[]{:S(2)}) async-start(), calls=%async_computation.12 | async-start | bytes 1064960 | tf_op jit(solution)/shard_map/all_gather | solution.py:99
  26.9 714.5 %reduce-scatter.13.cloned.1.call-start = ((), (), s32[]{:S(2)}) async-start(), calls=%async_computation.13 | async-start | bytes 589824
  86.2 399.2 %copy-start.4 = (bf16[64,64]{1,0:T(8,128)(2,1)S(1)}, bf16[64,64]{1,0:T(8,128)(2,1)}, u32[]{:S(2)}) copy-start(bf16[64,64]{1,0:T(8,128)(2,1)} %param.27) | copy-start | bytes 24580
  86.2 399.2 %copy-start.8 = (f32[64]{0:T(128)S(1)}, f32[64]{0:T(128)}, u32[]{:S(2)}) copy-start(f32[64]{0:T(128)} %param.28) | copy-start | bytes 772
  489.4 2.5 copy-start.6
  489.5 2.5 copy-start.12
  489.5 2.5 copy-start.20
  491.9 2.4 copy-start.11
  491.9 2.4 copy-start.22
  496.6 1.4 copy-start.14
  496.6 1.4 copy-start.18
  497.7 2.7 copy-start.13
  497.7 2.7 copy-start.19
  497.7 284.3 %reduce-scatter.15.cloned.1.call-start = ((), (), s32[]{:S(2)}) async-start(), calls=%async_computation.14 | async-start | bytes 589824
  500.4 2.4 copy-start.21
  502.8 2.4 copy-start.23
  508.6 313.8 %reduce-scatter.17.cloned.1.call-start = ((), (), s32[]{:S(2)}) async-start(), calls=%async_computation.15 | async-start | bytes 589824
  579.1 129.7 %copy-start.17 = (bf16[1024,1,512]{2,0,1:T(8,128)(2,1)S(1)}, bf16[1024,1,512]{2,0,1:T(8,128)(2,1)}, u32[]{:S(2)}) copy-start(bf16[1024,1,512]{2,0,1:T(8,128)(2,1)} %all-gather.12.cloned.1.call-done) | copy-start | bytes 3145732
  579.1 283.8 %reduce-scatter.19.cloned.1.call-start = ((), (), s32[]{:S(2)}) async-start(), calls=%async_computation.16 | async-start | bytes 589824
  864.5 1.6 copy-start.1
  864.5 1.6 copy-start.10
  868.2 1.9 copy-start.7
  870.1 2.3 copy-start.15
  870.1 2.3 copy-start.16
  1067.5 59.7 %all-to-all-start.3 = ((bf16[64,128,1,64]{1,3,2,0:T(8,128)(2,1)}), bf16[64,128,1,64]{1,3,2,0:T(8,128)(2,1)}, u32[]{:S(2)}, u32[]{:S(2)}) async-start(bf16[64,128,1,64]{1,3,2,0:T(8,128)(2,1)} %stack.15), calls=%async_computation.3 | async-start | bytes 2097152 | tf_op jit(solution)/shard_map/all_to_all | solution.py:13
  1073.6 1.2 copy-start.2
Sparse Core Ops, SparseCore 0:
  11.0 143.1 all-gather.7
  157.7 135.0 all-gather.5
  295.8 134.8 all-gather.9
  433.5 135.1 all-gather.11
  571.5 134.9 all-gather.13
  709.7 31.6 reduce-scatter.12
  744.4 37.5 reduce-scatter.14
  784.8 37.5 reduce-scatter.16
  825.4 37.5 reduce-scatter.18
